TPU v7x, 32 devices: a whole 2x2x4 slice. The times are simulated.
32 devices in a mesh: seq: 8 (over z, y), tp: 4 (over x, core).
Axes of the slice: x: 2, y: 2, z: 4, core: 2. Of those that a mesh axis runs over, the one named last changes fastest.
Arguments:
- tokens: bfloat16 [16384, 1024], P(('seq', 'tp')), may hold values from -6 to 6
- query_weight: bfloat16 [1024, 1024], replicated, may hold values from -0.1875 to 0.1875
- key_weight: bfloat16 [1024, 1024], replicated, may hold values from -0.1875 to 0.1875
- value_weight: bfloat16 [1024, 1024], replicated, may hold values from -0.1875 to 0.1875
- modulate_weight: bfloat16 [1024, 1024], replicated, may hold values from -0.1875 to 0.1875
- output_weight: bfloat16 [1024, 1024], replicated, may hold values from -0.1875 to 0.1875
- gate_weight: bfloat16 [1024, 2816], P(None, 'tp'), may hold values from -0.1875 to 0.1875
- linear_weight: bfloat16 [1024, 2816], P(None, 'tp'), may hold values from -0.1875 to 0.1875
- down_weight: bfloat16 [2816, 1024], P('tp'), may hold values from -0.109375 to 0.109375
- cotangent: bfloat16 [16384, 1024], P(('seq', 'tp')), may hold values from -6 to 6
- decay_exponent: int32 [8], replicated, may hold values from 5 to 17
Outputs:
- mixed: bfloat16 [16384, 1024], P(('seq', 'tp'))
- tokens_grad: float32 [16384, 1024], P(('seq', 'tp'))
- query_grad: float32 [1024, 1024], replicated
- key_grad: float32 [1024, 1024], replicated
- value_grad: float32 [1024, 1024], replicated
- modulate_grad: float32 [1024, 1024], replicated
- output_grad: float32 [1024, 1024], replicated
- gate_grad: float32 [1024, 2816], P('seq', 'tp')
- linear_grad: float32 [1024, 2816], P('seq', 'tp')
- down_grad: float32 [2816, 1024], P('tp', 'seq')
Inputs may be any that keep to these rules, and one draw needn't show every extreme that they name: `decay_exponent`: head h decays by a factor 2 ** (-2 ** (-decay_exponent_h)) a token.
All inputs are finite; a program needn't handle non-finite values.
Results may differ from a plain program's by a relative error of at most 0.015.
Values may be sent and summed in bfloat16 or wider, within the bound.
No kernel may reach another device: no remote copies, remote signals or barrier semaphores. Data moves between devices by JAX's collectives and lax.ppermute only.
A program may use at most 320 MiB of HBM per device.

v0:
```python
import math
import jax
import jax.numpy as jnp
from jax import lax
from jax.sharding import PartitionSpec as P

BLOCK = 256
SEQ_LEN = 16384
EPS = 1e-06
HIGH = lax.Precision.HIGHEST
FLOAT = jnp.float32
BHALF = jnp.bfloat16


def prefix(part, axis, combine, identity, reverse):
    count = lax.axis_size(axis)
    place = lax.axis_index(axis)
    ahead = count - 1 - place if reverse else place
    gathered = jax.tree.map(lambda a: lax.all_gather(a, axis), part)
    state = jax.tree.map(lambda a, e: jnp.zeros_like(a) + jnp.asarray(e, a.dtype), part, identity)

    def one(lap, state):
        source = count - 1 - lap if reverse else lap
        return combine(
            state, jax.tree.map(lambda a: lax.dynamic_index_in_dim(a, source, 0, False), gathered)
        )

    return lax.fori_loop(0, ahead, one, state)


def srms(values):
    return values * lax.rsqrt(jnp.mean(values * values, axis=-1, keepdims=True) + EPS)


def srms_back(values, gradient):
    scaled = lax.rsqrt(jnp.mean(values * values, axis=-1, keepdims=True) + EPS)
    normed = values * scaled
    return scaled * (gradient - normed * jnp.mean(gradient * normed, axis=-1, keepdims=True))


def swish(values):
    return values * jax.nn.sigmoid(values)


def swish_slope(values):
    sigmoid = jax.nn.sigmoid(values)
    return sigmoid * (1.0 + values * (1.0 - sigmoid))


def angles(position, halves):
    column = jnp.arange(halves, dtype=jnp.int32)
    factor = 1 + jnp.right_shift(jnp.full((halves,), 16384, jnp.int32), column // 4)
    phase = position[:, None] * factor[None, :] % 65536
    turned = phase.astype(jnp.float32) * (2.0 * math.pi / 65536.0)
    return (jnp.cos(turned)[:, None, :], jnp.sin(turned)[:, None, :])


def rotate(values, cosine, sine):
    halves = values.shape[-1] // 2
    first = values[..., :halves]
    second = values[..., halves:]
    return jnp.concatenate(
        [first * cosine - second * sine, first * sine + second * cosine], axis=-1
    )


def unrotate(values, cosine, sine):
    halves = values.shape[-1] // 2
    first = values[..., :halves]
    second = values[..., halves:]
    return jnp.concatenate(
        [first * cosine + second * sine, second * cosine - first * sine], axis=-1
    )


def combine(earlier, latter):
    return (earlier[0] * latter[0], latter[0][:, None, None] * earlier[1] + latter[1])


def matmul(left, right):
    return jnp.dot(left, right, preferred_element_type=FLOAT)


def contract_rows(left, right):
    return lax.dot_general(left, right, (((0,), (0,)), ((), ())), preferred_element_type=FLOAT)


def contract_cols(left, right):
    return lax.dot_general(left, right, (((1,), (1,)), ((), ())), preferred_element_type=FLOAT)


def shards(
    tokens,
    query_weight,
    key_weight,
    value_weight,
    modulate_weight,
    output_weight,
    gate_weight,
    linear_weight,
    down_weight,
    cotangent,
    decay_exponent,
):
    tok_count, width = tokens.shape
    heads = decay_exponent.shape[0]
    head_dim = width // heads
    devices = lax.axis_size("seq") * lax.axis_size("tp")
    seq_length = min(SEQ_LEN, tok_count * devices)
    device_place = lax.axis_index("seq") * lax.axis_size("tp") + lax.axis_index("tp")
    first_token = device_place * tok_count
    position = (first_token + jnp.arange(tok_count, dtype=jnp.int32)) % seq_length
    is_start = first_token % seq_length == 0
    decay_rate = jnp.exp2(-decay_exponent.astype(FLOAT))
    cosine, sine = angles(position, head_dim // 2)
    offsets = jnp.arange(BLOCK, dtype=FLOAT)
    distance = offsets[:, None] - offsets[None, :]
    decay_matrix = jnp.where(
        distance[None] >= 0.0,
        jnp.exp2(-jnp.maximum(distance, 0.0)[None] * decay_rate[:, None, None]),
        0.0,
    )
    query_decay = jnp.exp2(-(offsets + 1.0)[:, None] * decay_rate[None, :])[:, :, None]
    key_decay = jnp.exp2(-(BLOCK - 1.0 - offsets)[:, None] * decay_rate[None, :])[:, :, None]
    block_decay = jnp.exp2(-BLOCK * decay_rate)[:, None, None]
    device_decay = jnp.where(is_start, 0.0, jnp.exp2(-tok_count * decay_rate))
    blocks = tok_count // BLOCK
    inputs = tokens.astype(FLOAT)
    normed = srms(inputs).astype(BHALF)
    pre_query = matmul(normed, query_weight)
    pre_key = matmul(normed, key_weight)
    modulate = matmul(normed, modulate_weight)
    query = rotate(swish(pre_query).reshape(tok_count, heads, head_dim), cosine, sine).astype(BHALF)
    keys = rotate(swish(pre_key).reshape(tok_count, heads, head_dim), cosine, sine).astype(BHALF)
    values = matmul(normed, value_weight).astype(BHALF).reshape(tok_count, heads, head_dim)
    key_states = []
    decayed_queries = []
    decayed_keys = []
    local_state = jnp.zeros((heads, head_dim, head_dim), FLOAT)
    for number in range(blocks):
        window = slice(number * BLOCK, (number + 1) * BLOCK)
        decayed_key = (keys[window].astype(FLOAT) * key_decay).astype(BHALF)
        decayed_query = (query[window].astype(FLOAT) * query_decay).astype(BHALF)
        decayed_keys.append(decayed_key)
        decayed_queries.append(decayed_query)
        contrib = jnp.einsum(
            "jhd,jhe->hde", decayed_key, values[window], preferred_element_type=FLOAT
        )
        key_states.append(contrib)
        local_state = block_decay * local_state + contrib
    identity = (jnp.ones_like(device_decay), jnp.zeros_like(local_state))
    carried = prefix((device_decay, local_state), ("seq", "tp"), combine, identity, False)
    state = jnp.where(is_start, 0.0, carried[1])
    pieces = []
    used_states = []
    for number in range(blocks):
        window = slice(number * BLOCK, (number + 1) * BLOCK)
        block_query = query[window]
        scores = jnp.einsum("ihd,jhd->hij", block_query, keys[window], preferred_element_type=FLOAT)
        probs = (scores * decay_matrix).astype(BHALF)
        intra = jnp.einsum("hij,jhd->ihd", probs, values[window], preferred_element_type=FLOAT)
        state_used = state.astype(BHALF)
        inter = jnp.einsum(
            "ihd,hde->ihe", decayed_queries[number], state_used, preferred_element_type=FLOAT
        )
        used_states.append(state_used)
        state = block_decay * state + key_states[number]
        pieces.append(intra + inter)
    attended = jnp.concatenate(pieces, axis=0).reshape(tok_count, width)
    normed_out = srms(attended)
    gated = (normed_out * modulate).astype(BHALF)
    resid = inputs + matmul(gated, output_weight)
    normed_two = srms(resid).astype(BHALF)
    gathered = lax.all_gather(normed_two, "tp", axis=0, tiled=True)
    gate_pre = matmul(gathered, gate_weight)
    linear_pre = matmul(gathered, linear_weight)
    hidden = (gate_pre * linear_pre).astype(BHALF)
    feed = lax.psum_scatter(
        matmul(hidden, down_weight).astype(jnp.bfloat16), "tp", scatter_dimension=0, tiled=True
    ).astype(jnp.float32)
    mixed = (resid + feed).astype(BHALF)
    cot_rows = lax.all_gather(cotangent, "tp", axis=0, tiled=True)
    down_part = contract_rows(hidden, cot_rows)
    hidden_cot = contract_cols(cot_rows, down_weight)
    gate_back = (hidden_cot * linear_pre).astype(BHALF)
    linear_back = (hidden_cot * gate_pre).astype(BHALF)
    gate_part = contract_rows(gathered, gate_back)
    linear_part = contract_rows(gathered, linear_back)
    normed_cot = lax.psum_scatter(
        contract_cols(gate_back, gate_weight) + contract_cols(linear_back, linear_weight),
        "tp",
        scatter_dimension=0,
        tiled=True,
    )
    gate_grad, linear_grad, down_grad = (
        lax.psum_scatter(
            gate_part.astype(jnp.bfloat16), "seq", scatter_dimension=0, tiled=True
        ).astype(jnp.float32),
        lax.psum_scatter(
            linear_part.astype(jnp.bfloat16), "seq", scatter_dimension=0, tiled=True
        ).astype(jnp.float32),
        lax.psum_scatter(
            down_part.astype(jnp.bfloat16), "seq", scatter_dimension=1, tiled=True
        ).astype(jnp.float32),
    )
    resid_cot = cotangent.astype(FLOAT) + srms_back(resid, normed_cot)
    branch_back = resid_cot.astype(BHALF)
    output_part = contract_rows(gated, branch_back)
    gated_cot = contract_cols(branch_back, output_weight)
    modulate_back = (gated_cot * normed_out).astype(BHALF)
    attended_back = (
        srms_back(attended, gated_cot * modulate).astype(BHALF).reshape(tok_count, heads, head_dim)
    )
    direct = []
    for number in range(blocks):
        window = slice(number * BLOCK, (number + 1) * BLOCK)
        direct.append(
            jnp.einsum(
                "ihd,ihe->hde",
                decayed_queries[number],
                attended_back[window],
                preferred_element_type=FLOAT,
            )
        )
    inbound = jnp.zeros_like(local_state)
    for number in reversed(range(blocks)):
        inbound = block_decay * inbound + direct[number]
    masked = jnp.where(is_start, 0.0, inbound)
    after = prefix((device_decay, masked), ("seq", "tp"), combine, identity, True)
    outer = after[1]
    accum = jnp.zeros_like(local_state)
    query_parts = []
    key_parts = []
    value_parts = []
    for number in reversed(range(blocks)):
        window = slice(number * BLOCK, (number + 1) * BLOCK)
        state_cot = outer + accum
        outer = block_decay * outer
        accum = block_decay * accum + direct[number]
        block_query = query[window]
        block_key = keys[window]
        block_value = values[window]
        block_back = attended_back[window]
        key_part = (
            jnp.einsum("hde,jhe->jhd", state_cot, block_value.astype(FLOAT), precision=HIGH)
            * key_decay
        )
        value_part = jnp.einsum(
            "jhd,hde->jhe", decayed_keys[number].astype(FLOAT), state_cot, precision=HIGH
        )
        scores = jnp.einsum("ihd,jhd->hij", block_query, block_key, preferred_element_type=FLOAT)
        probs = (scores * decay_matrix).astype(BHALF)
        prob_cot = jnp.einsum("ihe,jhe->hij", block_back, block_value, preferred_element_type=FLOAT)
        score_back = (prob_cot * decay_matrix).astype(BHALF)
        value_part = value_part + jnp.einsum(
            "hij,ihe->jhe", probs, block_back, preferred_element_type=FLOAT
        )
        key_part = key_part + jnp.einsum(
            "hij,ihd->jhd", score_back, block_query, preferred_element_type=FLOAT
        )
        query_part = jnp.einsum("hij,jhd->ihd", score_back, block_key, preferred_element_type=FLOAT)
        query_part = (
            query_part
            + jnp.einsum(
                "ihe,hde->ihd", block_back, used_states[number], preferred_element_type=FLOAT
            )
            * query_decay
        )
        query_parts.insert(0, query_part)
        key_parts.insert(0, key_part)
        value_parts.insert(0, value_part)
    query_cot = jnp.concatenate(query_parts, axis=0)
    key_cot = jnp.concatenate(key_parts, axis=0)
    value_cot = jnp.concatenate(value_parts, axis=0)
    query_back = (
        unrotate(query_cot, cosine, sine).reshape(tok_count, width) * swish_slope(pre_query)
    ).astype(BHALF)
    key_back = (
        unrotate(key_cot, cosine, sine).reshape(tok_count, width) * swish_slope(pre_key)
    ).astype(BHALF)
    value_back = value_cot.reshape(tok_count, width).astype(BHALF)
    normed_grad = contract_cols(query_back, query_weight) + contract_cols(key_back, key_weight)
    normed_grad = (
        normed_grad
        + contract_cols(value_back, value_weight)
        + contract_cols(modulate_back, modulate_weight)
    )
    tokens_grad = resid_cot + srms_back(inputs, normed_grad)
    query_grad, key_grad, value_grad, modulate_grad, output_grad = lax.psum(
        (
            contract_rows(normed, query_back),
            contract_rows(normed, key_back),
            contract_rows(normed, value_back),
            contract_rows(normed, modulate_back),
            output_part,
        ),
        ("seq", "tp"),
    )
    return (
        mixed,
        tokens_grad,
        query_grad,
        key_grad,
        value_grad,
        modulate_grad,
        output_grad,
        gate_grad,
        linear_grad,
        down_grad,
    )


def solution(mesh):
    return jax.shard_map(
        shards,
        mesh=mesh,
        in_specs=(
            P(("seq", "tp"), None),
            P(),
            P(),
            P(),
            P(),
            P(),
            P(None, "tp"),
            P(None, "tp"),
            P("tp", None),
            P(("seq", "tp"), None),
            P(),
        ),
        out_specs=(
            P(("seq", "tp"), None),
            P(("seq", "tp"), None),
            P(),
            P(),
            P(),
            P(),
            P(),
            P("seq", "tp"),
            P("seq", "tp"),
            P("tp", "seq"),
        ),
        check_vma=False,
    )
```

profile of v0, /device:TPU:0, one launch (start us, length us, event | category | flops | bytes accessed | tf_op | source)
XLA Modules:
  0.0 1147.0 jit_solution(10695310475397209086)
XLA Ops:
  9.7 3.3 convolution_convert_fusion.4
  26.5 5.1 subtract_convert_fusion
  37.9 42.9 %all-reduce = f32[256]{0:T(256)S(1)} all-reduce(f32[256]{0:T(256)S(1)} %get-tuple-element.206), channel_id=2, replica_groups=mesh['seq'=8,'tp'=4] {'seq','tp'}, use_global_device_ids=true, to_apply=%add | all-reduce | flops 256 | bytes 2048
  87.4 69.5 %all-gather.12.cloned.1.call-done = f32[256,128,128]{2,1,0:T(8,128)} async-done(((f32[8,128,128]{2,1,0:T(8,128)}), f32[256,128,128]{2,1,0:T(8,128)}) %all-gather.12.cloned.1.call-update) | async-done | bytes 16777232 | tf_op jit(solution)/shard_map/all_gather | solution.py:19
  166.5 4.8 multiply_convert_fusion.7
  176.1 98.1 %all-gather.8.cloned.1.call-done = bf16[2048,1024]{1,0:T(8,128)(2,1)} async-done(((bf16[512,1024]{1,0:T(8,128)(2,1)}), bf16[2048,1024]{1,0:T(8,128)(2,1)}) %all-gather.8.cloned.1.call-update) | async-done | bytes 4194320 | tf_op jit(solution)/shard_map/all_gather | solution.py:174
  274.3 8.4 fusion.83
  282.7 5.1 fusion.82
  287.8 22.6 %all-gather.10.cloned.1.call-done = bf16[2048,1024]{1,0:T(8,128)(2,1)} async-done(((bf16[512,1024]{1,0:T(8,128)(2,1)}), bf16[2048,1024]{1,0:T(8,128)(2,1)}) %all-gather.10.cloned.1.call-update) | async-done | bytes 4194320 | tf_op jit(solution)/shard_map/all_gather | solution.py:182
  310.3 11.0 multiply_convert_fusion
  321.4 3.5 fusion.84
  324.9 6.0 convolution_add_fusion
  331.2 7.7 convolution_convert_fusion
  339.0 63.8 %reduce-scatter.14.cloned.1.call-done = f32[512,1024]{1,0:T(8,128)} async-done(((f32[2048,1024]{1,0:T(8,128)}), f32[512,1024]{1,0:T(8,128)}) %reduce-scatter.14.cloned.1.call-update) | async-done | bytes 2097168 | tf_op jit(solution)/shard_map/reduce_scatter | solution.py:189
  405.4 45.1 %reduce-scatter.12.cloned.1.call-done = bf16[512,1024]{1,0:T(8,128)(2,1)} async-done(((bf16[2048,1024]{1,0:T(8,128)(2,1)}), bf16[512,1024]{1,0:T(8,128)(2,1)}) %reduce-scatter.12.cloned.1.call-update) | async-done | bytes 1048592 | tf_op jit(solution)/shard_map/reduce_scatter | solution.py:178
  450.5 4.5 multiply_add_fusion.2
  464.8 7.3 convolution_convert_fusion.3
  475.3 7.3 convolution_convert_fusion.1
  485.3 7.3 convolution_convert_fusion.2
  502.4 3.3 fusion.38
  508.8 3.4 fusion.64
  512.2 67.6 %all-gather.14.cloned.1.call-done = f32[256,128,128]{2,1,0:T(8,128)} async-done(((f32[8,128,128]{2,1,0:T(8,128)}), f32[256,128,128]{2,1,0:T(8,128)}) %all-gather.14.cloned.1.call-update) | async-done | bytes 16777232 | tf_op jit(solution)/shard_map/all_gather | solution.py:19
  579.8 38.5 %while.27 = (s32[]{:T(128)}, f32[8,128,128]{2,1,0:T(8,128)S(1)}, s32[]{:T(128)}, f32[32,8]{1,0:T(8,128)S(1)}, f32[32,8,128,128]{3,2,1,0:T(8,128)}, /*index=5*/s32[]{:T(128)}, s32[]{:T(128)}, s32[]{:T(128)}, s32[]{:T(128)}) while((s32[]{:T(128)}, f32[8,128,128]{2,1,0:T(8,128)S(1)}, s32[]{:T(128)}, f32[32,8]{1,0:T(8,128)S(1)}, ...), condition=%wide.region_10.11_spmd, body=%wide.region_9.10_spmd.sunk | while | flops 262150 | bytes 1573115 | solution.py:28
  627.2 3.5 fusion.66
  633.3 3.4 fusion.70
  638.6 3.4 fusion.68
  642.0 4.3 reduce-scatter.20.cloned.1.call-done
  648.2 65.8 %reduce-scatter.18.cloned.1.call-done = bf16[128,704]{1,0:T(8,128)(2,1)} async-done(((bf16[1024,704]{1,0:T(8,128)(2,1)}), bf16[128,704]{1,0:T(8,128)(2,1)}) %reduce-scatter.18.cloned.1.call-update) | async-done | bytes 180240
  715.8 66.0 %reduce-scatter.16.cloned.1.call-done = bf16[128,704]{1,0:T(8,128)(2,1)} async-done(((bf16[1024,704]{1,0:T(8,128)(2,1)}), bf16[128,704]{1,0:T(8,128)(2,1)}) %reduce-scatter.16.cloned.1.call-update) | async-done | bytes 180240
  783.7 3.0 fusion.87
  794.0 326.8 %all-reduce.4.cloned.1.call-done = (f32[1024,1024]{1,0:T(8,128)}, f32[1024,1024]{1,0:T(8,128)}, f32[1024,1024]{1,0:T(8,128)}, f32[1024,1024]{1,0:T(8,128)}, f32[1024,1024]{1,0:T(8,128)}) async-done(((f32[1024,1024]{1,0:T(8,128)}, f32[1024,1024]{1,0:T(8,128)}, f32[1024,1024]{1,0:T(8,128)}, f32[1024,1024]{1,0:T(8,128)}, f32[1024,1024]{1,0:T(8,128)}), (f32[1024,1024]{1,0:T(8,128)}, f32[1024,1024]{1,0:T(8,128)}, ...) | async-done | bytes 20971536 | tf_op jit(solution)/shard_map/psum | solution.py:289
  1120.8 4.9 copy.240
  (333 shorter events, 151.5 us)
Async XLA Ops:
  7.2 164.2 %copy-start = (bf16[1024,1024]{1,0:T(8,128)(2,1)S(1)}, bf16[1024,1024]{1,0:T(8,128)(2,1)}, u32[]{:S(2)}) copy-start(bf16[1024,1024]{1,0:T(8,128)(2,1)} %param.20) | copy-start | bytes 6291460
  7.2 149.7 %all-gather.12.cloned.1.call-start = ((), (), s32[]{:S(2)}) async-start(), calls=%async_computation.9 | async-start | bytes 17301504 | tf_op jit(solution)/shard_map/all_gather | solution.py:19
  9.6 4.4 copy-start.2
  9.6 4.4 copy-start.77
  25.8 5.8 copy-start.66
  31.6 4.6 copy-start.36
  37.8 236.5 %all-gather.8.cloned.1.call-start = ((), (), s32[]{:S(2)}) async-start(), calls=%async_computation.5 | async-start | bytes 5242880 | tf_op jit(solution)/shard_map/all_gather | solution.py:174
  175.2 135.2 %all-gather.10.cloned.1.call-start = ((), (), s32[]{:S(2)}) async-start(), calls=%async_computation.7 | async-start | bytes 5242880 | tf_op jit(solution)/shard_map/all_gather | solution.py:182
  175.9 226.9 %reduce-scatter.14.cloned.1.call-start = ((), (), s32[]{:S(2)}) async-start(), calls=%async_computation.8 | async-start | bytes 10485760 | tf_op jit(solution)/shard_map/reduce_scatter | solution.py:189
  274.3 8.4 copy-start.74
  274.3 8.4 copy-start.79
  310.3 11.0 copy-start.80
  321.4 3.5 copy-start.14
  321.4 3.5 copy-start.15
  321.4 3.5 copy-start.81
  330.9 119.5 %reduce-scatter.12.cloned.1.call-start = ((), (), s32[]{:S(2)}) async-start(), calls=%async_computation.6 | async-start | bytes 5242880 | tf_op jit(solution)/shard_map/reduce_scatter | solution.py:178
  339.0 240.8 %all-gather.14.cloned.1.call-start = ((), (), s32[]{:S(2)}) async-start(), calls=%async_computation.10 | async-start | bytes 17301504 | tf_op jit(solution)/shard_map/all_gather | solution.py:19
  450.5 4.5 copy-start.3
  450.5 4.5 copy-start.9
  459.1 39.9 %copy-start.40 = (bf16[256,1024]{0,1:T(8,128)(2,1)}, bf16[256,1024]{0,1:T(8,128)(2,1)S(1)}, u32[]{:S(2)}) copy-start(bf16[256,1024]{0,1:T(8,128)(2,1)S(1)} %copy.173) | copy-start | bytes 1572868
  462.0 33.3 %copy-start.44 = (bf16[256,1024]{0,1:T(8,128)(2,1)}, bf16[256,1024]{0,1:T(8,128)(2,1)S(1)}, u32[]{:S(2)}) copy-start(bf16[256,1024]{0,1:T(8,128)(2,1)S(1)} %copy.172) | copy-start | bytes 1572868
  464.8 181.6 %reduce-scatter.20.cloned.1.call-start = ((), (), s32[]{:S(2)}) async-start(), calls=%async_computation.13 | async-start | bytes 1769472
  474.8 239.2 %reduce-scatter.18.cloned.1.call-start = ((), (), s32[]{:S(2)}) async-start(), calls=%async_computation.12 | async-start | bytes 1769472
  485.3 296.6 %reduce-scatter.16.cloned.1.call-start = ((), (), s32[]{:S(2)}) async-start(), calls=%async_computation.11 | async-start | bytes 1769472
  495.3 625.5 %all-reduce.4.cloned.1.call-start = ((), (), s32[]{:S(2)}) async-start(), calls=%async_computation.14 | async-start | bytes 41943040 | tf_op jit(solution)/shard_map/psum | solution.py:289
  579.8 38.5 %copy-start.22 = (bf16[256,8,128]{2,0,1:T(8,128)(2,1)S(1)}, bf16[256,8,128]{2,0,1:T(8,128)(2,1)}, u32[]{:S(2)}) copy-start(bf16[256,8,128]{2,0,1:T(8,128)(2,1)} %copy-done.20) | copy-start | bytes 1572868
  627.2 3.5 copy-start.67
  642.0 141.7 %copy-start.71 = (bf16[512,8,128]{0,2,1:T(8,128)(2,1)S(1)}, bf16[512,8,128]{0,2,1:T(8,128)(2,1)}, u32[]{:S(2)}) copy-start(bf16[512,8,128]{0,2,1:T(8,128)(2,1)} %copy-done.70) | copy-start | bytes 3145732
  1120.8 4.9 copy-start.62
  1125.8 3.7 copy-start.61
  1129.5 3.7 copy-start.60
  1133.2 3.7 copy-start.59
  (60 other events, 124.8 us)
Sparse Core Ops, SparseCore 0:
  37.9 118.8 all-gather.11
  175.3 98.9 all-gather.7
  275.8 34.4 all-gather.9
  331.1 71.7 reduce-scatter.13
  405.9 44.5 reduce-scatter.11
  464.9 114.8 all-gather.13
  583.2 63.0 reduce-scatter.19
  650.1 63.7 reduce-scatter.17
  718.0 63.8 reduce-scatter.15
  789.8 330.9 all-reduce.3
where the time goes:
time: 1160 us; the launch traced here: 1150 us
  waiting for transfers between devices  831 us (72%)
  matrix products  132 us (11%)
  other arithmetic  68.9 us (6%)
  local copies, waits for them, and re-layouts  54.8 us (5%)
  blocking collectives  42.9 us (4%)
  between operations  15.3 us (1%)
    psum x1, waiting for transfers between devices, shards(): lax.psum((contract_rows(normed, query_back), contract_rows(normed, key_ba...  327 us
    all_gather x2, waiting for transfers between devices, prefix(): gathered = jax.tree.map(lambda a: lax.all_gather(a, axis), part)  137 us
    unnamed x13, waiting for transfers between devices  137 us
    all_gather x1, waiting for transfers between devices, shards(): gathered = lax.all_gather(normed_two, 'tp', axis=0, tiled=True)  98.1 us
    reduce_scatter x1, waiting for transfers between devices, shards(): lax.psum_scatter(contract_cols(gate_back, gate_weight) + contract_cols(li...  63.8 us
    reduce_scatter x1, waiting for transfers between devices, shards(): lax.psum_scatter(matmul(hidden, down_weight).astype(jnp.bfloat16), 'tp',...  45.1 us
    unnamed x179, local copies, waits for them, and re-layouts  43 us
    unnamed x1, blocking collectives  42.9 us
  transfers between devices with their start and end apart: 10, of which 10 were waited for; matrix products, arithmetic and copies ran while one was open for 13% of the time, Pallas kernels for 0%

commit v1 on v0

--- a/solution.py
+++ b/solution.py
@@ -1,3 +1,4 @@
+import functools
 import math
 import jax
 import jax.numpy as jnp
@@ -10,6 +11,14 @@
 HIGH = lax.Precision.HIGHEST
 FLOAT = jnp.float32
 BHALF = jnp.bfloat16
+
+
+def bind_the_sector(work_x, along_axis, shard_axis):
+    taken_in = lax.psum(lax.psum(work_x, along_axis), shard_axis)
+    return taken_in
+
+
+use_pools_here = functools.partial(bind_the_sector, along_axis="tp", shard_axis="seq")
 
 
 def prefix(part, axis, combine, identity, reverse):
@@ -286,15 +295,14 @@
         + contract_cols(modulate_back, modulate_weight)
     )
     tokens_grad = resid_cot + srms_back(inputs, normed_grad)
-    query_grad, key_grad, value_grad, modulate_grad, output_grad = lax.psum(
+    query_grad, key_grad, value_grad, modulate_grad, output_grad = use_pools_here(
         (
             contract_rows(normed, query_back),
             contract_rows(normed, key_back),
             contract_rows(normed, value_back),
             contract_rows(normed, modulate_back),
             output_part,
-        ),
-        ("seq", "tp"),
+        )
     )
     return (
         mixed,

time: 1160 us -> 1870 us (1.61)
  waiting for transfers between devices: 831 us -> 1550 us
    psum x1 -> x2, waiting for transfers between devices: 327 us -> 951 us  [bind_the_sector(): taken_in = lax.psum(lax.psum(work_x, along_axis), shard_axis)]
    unnamed x13 -> x14, waiting for transfers between devices: 137 us -> 201 us
    all_gather x2, waiting for transfers between devices: 137 us -> 168 us  [prefix(): gathered = jax.tree.map(lambda a: lax.all_gather(a, axis), part)]
    unnamed x179 -> x177, local copies, waits for them, and re-layouts: 43 us -> 40.5 us
  transfers between devices with their start and end apart: 10 -> 11, of which waited for: 10 -> 11; matrix products, arithmetic and copies ran while one was open for 13% -> 5% of each run, Pallas kernels for 0% -> 0%
where the time goes in v1:
time: 1870 us; the launch traced here: 1860 us
  waiting for transfers between devices  1550 us (83%)
  matrix products  130 us (7%)
  other arithmetic  68.8 us (4%)
  local copies, waits for them, and re-layouts  53.6 us (3%)
  blocking collectives  42.9 us (2%)
    psum x2, waiting for transfers between devices, bind_the_sector(): taken_in = lax.psum(lax.psum(work_x, along_axis), shard_axis)  951 us
    unnamed x14, waiting for transfers between devices  201 us
    all_gather x2, waiting for transfers between devices, prefix(): gathered = jax.tree.map(lambda a: lax.all_gather(a, axis), part)  168 us
    all_gather x1, waiting for transfers between devices, shards(): gathered = lax.all_gather(normed_two, 'tp', axis=0, tiled=True)  97.8 us
    reduce_scatter x1, waiting for transfers between devices, shards(): lax.psum_scatter(contract_cols(gate_back, gate_weight) + contract_cols(li...  63.6 us
    reduce_scatter x1, waiting for transfers between devices, shards(): lax.psum_scatter(matmul(hidden, down_weight).astype(jnp.bfloat16), 'tp',...  45.1 us
    unnamed x1, blocking collectives  42.9 us
    unnamed x177, local copies, waits for them, and re-layouts  40.5 us
  transfers between devices with their start and end apart: 11, of which 11 were waited for; matrix products, arithmetic and copies ran while one was open for 5% of the time, Pallas kernels for 0%

profile of v1, /device:TPU:0, one launch (start us, length us, event | category | flops | bytes accessed | tf_op | source)
XLA Modules:
  0.0 1863.1 jit_solution(17924168015565770929)
XLA Ops:
  9.7 3.3 convolution_convert_fusion.4
  26.4 5.1 subtract_convert_fusion
  37.9 42.9 %all-reduce = f32[256]{0:T(256)S(1)} all-reduce(f32[256]{0:T(256)S(1)} %get-tuple-element.211), channel_id=2, replica_groups=mesh['seq'=8,'tp'=4] {'seq','tp'}, use_global_device_ids=true, to_apply=%add | all-reduce | flops 256 | bytes 2048
  87.4 69.5 %all-gather.12.cloned.1.call-done = f32[256,128,128]{2,1,0:T(8,128)} async-done(((f32[8,128,128]{2,1,0:T(8,128)}), f32[256,128,128]{2,1,0:T(8,128)}) %all-gather.12.cloned.1.call-update) | async-done | bytes 16777232 | tf_op jit(solution)/shard_map/all_gather | solution.py:28
  166.5 4.8 multiply_convert_fusion.7
  176.1 97.8 %all-gather.8.cloned.1.call-done = bf16[2048,1024]{1,0:T(8,128)(2,1)} async-done(((bf16[512,1024]{1,0:T(8,128)(2,1)}), bf16[2048,1024]{1,0:T(8,128)(2,1)}) %all-gather.8.cloned.1.call-update) | async-done | bytes 4194320 | tf_op jit(solution)/shard_map/all_gather | solution.py:183
  274.0 8.4 fusion.83
  282.4 5.0 fusion.82
  287.4 22.7 %all-gather.10.cloned.1.call-done = bf16[2048,1024]{1,0:T(8,128)(2,1)} async-done(((bf16[512,1024]{1,0:T(8,128)(2,1)}), bf16[2048,1024]{1,0:T(8,128)(2,1)}) %all-gather.10.cloned.1.call-update) | async-done | bytes 4194320 | tf_op jit(solution)/shard_map/all_gather | solution.py:191
  310.1 11.0 multiply_convert_fusion
  321.1 3.5 fusion.84
  324.6 6.0 convolution_add_fusion
  331.1 7.7 convolution_convert_fusion
  338.9 63.6 %reduce-scatter.14.cloned.1.call-done = f32[512,1024]{1,0:T(8,128)} async-done(((f32[2048,1024]{1,0:T(8,128)}), f32[512,1024]{1,0:T(8,128)}) %reduce-scatter.14.cloned.1.call-update) | async-done | bytes 2097168 | tf_op jit(solution)/shard_map/reduce_scatter | solution.py:198
  405.1 45.1 %reduce-scatter.12.cloned.1.call-done = bf16[512,1024]{1,0:T(8,128)(2,1)} async-done(((bf16[2048,1024]{1,0:T(8,128)(2,1)}), bf16[512,1024]{1,0:T(8,128)(2,1)}) %reduce-scatter.12.cloned.1.call-update) | async-done | bytes 1048592 | tf_op jit(solution)/shard_map/reduce_scatter | solution.py:187
  450.2 4.5 multiply_add_fusion.2
  476.2 3.4 fusion.64
  479.7 3.3 fusion.38
  483.0 98.5 %all-gather.14.cloned.1.call-done = f32[256,128,128]{2,1,0:T(8,128)} async-done(((f32[8,128,128]{2,1,0:T(8,128)}), f32[256,128,128]{2,1,0:T(8,128)}) %all-gather.14.cloned.1.call-update) | async-done | bytes 16777232 | tf_op jit(solution)/shard_map/all_gather | solution.py:28
  581.6 38.4 %while.27 = (s32[]{:T(128)}, f32[8,128,128]{2,1,0:T(8,128)S(1)}, s32[]{:T(128)}, f32[32,8]{1,0:T(8,128)S(1)}, f32[32,8,128,128]{3,2,1,0:T(8,128)}, /*index=5*/s32[]{:T(128)}, s32[]{:T(128)}, s32[]{:T(128)}, s32[]{:T(128)}) while((s32[]{:T(128)}, f32[8,128,128]{2,1,0:T(8,128)S(1)}, s32[]{:T(128)}, f32[32,8]{1,0:T(8,128)S(1)}, ...), condition=%wide.region_10.11_spmd, body=%wide.region_9.10_spmd.sunk | while | flops 262150 | bytes 1573115 | solution.py:37
  628.8 3.5 fusion.66
  634.9 3.4 fusion.70
  640.2 3.4 fusion.68
  643.9 7.5 convolution_convert_fusion.3
  653.0 6.3 convolution_convert_fusion.1
  661.0 6.3 convolution_convert_fusion.2
  669.2 328.9 %all-reduce.8.cloned.1.call-done = (f32[1024,1024]{1,0:T(8,128)}, f32[1024,1024]{1,0:T(8,128)}, f32[1024,1024]{1,0:T(8,128)}, f32[1024,1024]{1,0:T(8,128)}, f32[1024,1024]{1,0:T(8,128)}) async-done(((f32[1024,1024]{1,0:T(8,128)}, f32[1024,1024]{1,0:T(8,128)}, f32[1024,1024]{1,0:T(8,128)}, f32[1024,1024]{1,0:T(8,128)}, f32[1024,1024]{1,0:T(8,128)}), (f32[1024,1024]{1,0:T(8,128)}, f32[1024,1024]{1,0:T(8,128)}, ...) | async-done | bytes 20971536 | tf_op jit(solution)/shard_map/psum | solution.py:17
  998.1 68.7 %reduce-scatter.20.cloned.1.call-done = bf16[128,704]{1,0:T(8,128)(2,1)} async-done(((bf16[1024,704]{1,0:T(8,128)(2,1)}), bf16[128,704]{1,0:T(8,128)(2,1)}) %reduce-scatter.20.cloned.1.call-update) | async-done | bytes 180240
  1068.6 65.3 %reduce-scatter.18.cloned.1.call-done = bf16[128,704]{1,0:T(8,128)(2,1)} async-done(((bf16[1024,704]{1,0:T(8,128)(2,1)}), bf16[128,704]{1,0:T(8,128)(2,1)}) %reduce-scatter.18.cloned.1.call-update) | async-done | bytes 180240
  1135.8 66.3 %reduce-scatter.16.cloned.1.call-done = bf16[128,704]{1,0:T(8,128)(2,1)} async-done(((bf16[1024,704]{1,0:T(8,128)(2,1)}), bf16[128,704]{1,0:T(8,128)(2,1)}) %reduce-scatter.16.cloned.1.call-update) | async-done | bytes 180240
  1214.9 622.2 %all-reduce.6.cloned.1.call-done = (f32[1024,1024]{1,0:T(8,128)}, f32[1024,1024]{1,0:T(8,128)}, f32[1024,1024]{1,0:T(8,128)}, f32[1024,1024]{1,0:T(8,128)}, f32[1024,1024]{1,0:T(8,128)}) async-done(((f32[1024,1024]{1,0:T(8,128)}, f32[1024,1024]{1,0:T(8,128)}, f32[1024,1024]{1,0:T(8,128)}, f32[1024,1024]{1,0:T(8,128)}, f32[1024,1024]{1,0:T(8,128)}), (f32[1024,1024]{1,0:T(8,128)}, f32[1024,1024]{1,0:T(8,128)}, ...) | async-done | bytes 20971536 | tf_op jit(solution)/shard_map/psum | solution.py:17
  1837.1 4.9 copy.245
  (334 shorter events, 153.7 us)
Async XLA Ops:
  7.2 164.1 %copy-start = (bf16[1024,1024]{1,0:T(8,128)(2,1)S(1)}, bf16[1024,1024]{1,0:T(8,128)(2,1)}, u32[]{:S(2)}) copy-start(bf16[1024,1024]{1,0:T(8,128)(2,1)} %param.20) | copy-start | bytes 6291460
  7.2 149.7 %all-gather.12.cloned.1.call-start = ((), (), s32[]{:S(2)}) async-start(), calls=%async_computation.9 | async-start | bytes 17301504 | tf_op jit(solution)/shard_map/all_gather | solution.py:28
  9.6 4.4 copy-start.2
  9.6 4.4 copy-start.76
  25.8 5.8 copy-start.65
  31.6 4.7 copy-start.35
  37.8 236.2 %all-gather.8.cloned.1.call-start = ((), (), s32[]{:S(2)}) async-start(), calls=%async_computation.5 | async-start | bytes 5242880 | tf_op jit(solution)/shard_map/all_gather | solution.py:183
  175.2 134.9 %all-gather.10.cloned.1.call-start = ((), (), s32[]{:S(2)}) async-start(), calls=%async_computation.7 | async-start | bytes 5242880 | tf_op jit(solution)/shard_map/all_gather | solution.py:191
  175.9 226.6 %reduce-scatter.14.cloned.1.call-start = ((), (), s32[]{:S(2)}) async-start(), calls=%async_computation.8 | async-start | bytes 10485760 | tf_op jit(solution)/shard_map/reduce_scatter | solution.py:198
  274.0 8.4 copy-start.73
  274.0 8.4 copy-start.78
  310.1 11.0 copy-start.79
  321.1 3.5 copy-start.14
  321.1 3.5 copy-start.15
  321.1 3.5 copy-start.80
  330.6 119.5 %reduce-scatter.12.cloned.1.call-start = ((), (), s32[]{:S(2)}) async-start(), calls=%async_computation.6 | async-start | bytes 5242880 | tf_op jit(solution)/shard_map/reduce_scatter | solution.py:187
  338.8 242.7 %all-gather.14.cloned.1.call-start = ((), (), s32[]{:S(2)}) async-start(), calls=%async_computation.10 | async-start | bytes 17301504 | tf_op jit(solution)/shard_map/all_gather | solution.py:28
  450.2 4.5 copy-start.3
  450.2 4.5 copy-start.9
  458.7 5.0 copy-start.34
  462.4 4.2 copy-start.28
  466.5 531.6 %all-reduce.8.cloned.1.call-start = ((), (), s32[]{:S(2)}) async-start(), calls=%async_computation.15 | async-start | bytes 41943040 | tf_op jit(solution)/shard_map/psum | solution.py:17
  581.6 38.4 %copy-start.22 = (bf16[256,8,128]{2,0,1:T(8,128)(2,1)S(1)}, bf16[256,8,128]{2,0,1:T(8,128)(2,1)}, u32[]{:S(2)}) copy-start(bf16[256,8,128]{2,0,1:T(8,128)(2,1)} %copy-done.20) | copy-start | bytes 1572868
  643.6 423.2 %reduce-scatter.20.cloned.1.call-start = ((), (), s32[]{:S(2)}) async-start(), calls=%async_computation.13 | async-start | bytes 1769472
  653.0 481.0 %reduce-scatter.18.cloned.1.call-start = ((), (), s32[]{:S(2)}) async-start(), calls=%async_computation.12 | async-start | bytes 1769472
  660.9 541.2 %reduce-scatter.16.cloned.1.call-start = ((), (), s32[]{:S(2)}) async-start(), calls=%async_computation.11 | async-start | bytes 1769472
  668.9 1168.2 %all-reduce.6.cloned.1.call-start = ((), (), s32[]{:S(2)}) async-start(), calls=%async_computation.14 | async-start | bytes 41943040 | tf_op jit(solution)/shard_map/psum | solution.py:17
  998.1 205.8 %copy-start.70 = (bf16[512,8,128]{0,2,1:T(8,128)(2,1)S(1)}, bf16[512,8,128]{0,2,1:T(8,128)(2,1)}, u32[]{:S(2)}) copy-start(bf16[512,8,128]{0,2,1:T(8,128)(2,1)} %copy-done.69) | copy-start | bytes 3145732
  1837.1 4.9 copy-start.61
  1842.0 3.7 copy-start.60
  1845.7 3.7 copy-start.59
  1849.5 3.7 copy-start.58
  (60 other events, 127.0 us)
Sparse Core Ops, SparseCore 0:
  37.9 118.8 all-gather.11
  175.3 98.6 all-gather.7
  275.5 34.4 all-gather.9
  330.8 71.6 reduce-scatter.13
  405.6 44.5 reduce-scatter.11
  466.6 114.8 all-gather.13
  643.7 354.3 all-reduce.7
  1001.9 64.8 reduce-scatter.19
  1070.2 63.7 reduce-scatter.17
  1138.2 63.8 reduce-scatter.15
  1207.3 629.7 all-reduce.5
